TPU v7x, 256 devices: a whole 4x4x8 slice. The times are simulated.
256 devices in a mesh: sub: 128 (over x_lo, y, z, core), row: 2 (over x_hi).
Axes of the slice: x: 4 (x_hi: 2, x_lo: 2; x = x_hi * 2 + x_lo), y: 4, z: 8, core: 2. Of those that a mesh axis runs over, the one named last changes fastest.
Arguments:
- compliance: bfloat16 [128, 36, 18, 128, 128], P('sub', 'row'), may hold values from -0.0625 to 0.0625
- block_columns: int32 [128, 36, 18], P('sub', 'row'), may hold values from 0 to 35, as said below
- load_response: bfloat16 [128, 32, 4608], P('sub', None, 'row'), may hold values from -6 to 6
- starting_motion: bfloat16 [128, 32, 4608], P('sub', None, 'row'), may hold values from -6 to 6
- start_traction: bfloat16 [128, 32, 4608], P('sub', None, 'row'), may hold values from -6 to 6
- stiffness: float32 [128, 4608], P('sub', 'row'), may hold values from 1 to 10
- history: float32 [128, 4608], P('sub', 'row'), may hold values from 0 to 0.6
- face_partner: int32 [128, 36], P('sub', 'row'), may hold values from -1 to 8, as said below
- orientation: int32 [128, 36, 128], P('sub', 'row'), may hold values from 0 to 127, as said below
Outputs:
- displacement: bfloat16 [128, 32, 4608], P('sub', None, 'row')
- traction: bfloat16 [128, 32, 4608], P('sub', None, 'row')
Inputs may be any that keep to these rules, and one draw needn't show every extreme that they name: `block_columns`: each block row names 18 distinct face columns. `face_partner`: an entry is -1 for a free face, else the position, within the facing group of the same run of the neighbouring substructure, of the matched face. Matches are mutual. Faces facing s+1 on the last substructure and faces facing s-1 on the first are free. In some run of some substructure all 9 faces facing s+1 are matched. `orientation`: each face's row is a permutation of 0 to 127; matched faces carry mutually inverse permutations.
All inputs are finite; a program needn't handle non-finite values.
Results may differ from a plain program's by a relative error of at most 0.0045.
The roundings to bfloat16 on the way count: a program that leaves them out, or rounds other values in their place, can miss the bound.
Values may be sent and summed in bfloat16 or wider, within the bound.
A program may use at most 64 MiB of HBM per device.

v0:
```python
import jax
import jax.numpy as jnp
from jax import lax
from jax.sharding import PartitionSpec as P

SURFACE_EXTENT = 128
ITERS = 3
search_stiffness = 1.0
onset_jump = 0.15
failure_jump = 1.5


def with_halo(cells, sides, width):
    for axis, dim in sides:
        count = lax.axis_size(axis)
        ends = count - 1
        head = lax.slice_in_dim(cells, 0, width, axis=dim)
        tail = lax.slice_in_dim(cells, cells.shape[dim] - width, cells.shape[dim], axis=dim)
        cells = jnp.concatenate(
            [
                lax.ppermute(tail, axis, [(i, (i + 1) % count) for i in range(ends)]),
                cells,
                lax.ppermute(head, axis, [((i + 1) % count, i) for i in range(ends)]),
            ],
            axis=dim,
        )
    return cells


def cohesive(upward_marker, constitutive_parameters, opposing_surface, live_mask):
    temporal_points = upward_marker.shape[0]
    mate_upward_marker = opposing_surface[:temporal_points]
    joint_rigidity = 0.5 * (constitutive_parameters[0] + opposing_surface[temporal_points])
    joint_record = jnp.maximum(constitutive_parameters[1], opposing_surface[temporal_points + 1])
    difference = upward_marker - mate_upward_marker
    jump_size = difference / (search_stiffness + 2.0 * joint_rigidity)
    running_peak = lax.associative_scan(jnp.maximum, jnp.abs(jump_size), axis=0)
    peak_jump = jnp.maximum(joint_record, running_peak)
    damage = jnp.clip((peak_jump - onset_jump) / (failure_jump - onset_jump), 0.0, 1.0)
    effective = joint_rigidity * (1.0 - damage)
    traction = jnp.where(
        live_mask, effective * difference / (search_stiffness + 2.0 * effective), 0.0
    )
    displacement = (traction - upward_marker) / search_stiffness
    return (displacement, traction)


def shards(
    compliance,
    block_columns,
    load_response,
    starting_motion,
    start_traction,
    stiffness,
    history,
    face_partner,
    orientation,
):
    compliance_rows = compliance[0]
    columns = block_columns[0]
    temporal_points = starting_motion.shape[1]
    segment_breadth = starting_motion.shape[2]
    number_surfaces = segment_breadth // SURFACE_EXTENT
    group_size = number_surfaces // 2
    stored_blocks = columns.shape[1]
    applied_forces = load_response[0].astype(jnp.float32)
    constitutive_parameters = jnp.stack([stiffness[0], history[0]]).reshape(
        2, number_surfaces, SURFACE_EXTENT
    )
    partner_table = face_partner[0]
    turning = orientation[0]
    turn_table = (
        turning[:, :, None] == jnp.arange(SURFACE_EXTENT, dtype=jnp.int32)[None, None, :]
    ).astype(jnp.float32)
    facing_up = jnp.arange(number_surfaces) < group_size
    live_mask = (partner_table >= 0)[:, None]
    safe_index = jnp.maximum(partner_table, 0)
    source = jnp.where(facing_up, safe_index, group_size + safe_index)
    present_motion = starting_motion[0].astype(jnp.float32)
    present_stress = start_traction[0].astype(jnp.float32)
    for iteration in range(ITERS):
        robin_sum = present_stress + search_stiffness * present_motion
        gathered_entries = lax.all_gather(robin_sum.astype(jnp.bfloat16), "row", axis=1, tiled=True)
        flexibility_tiles = gathered_entries.reshape(temporal_points, -1, SURFACE_EXTENT)

        def add_block(index, total):
            column_slice = lax.dynamic_index_in_dim(columns, index, 1, keepdims=False)
            piece = jnp.take(flexibility_tiles, column_slice, axis=1)
            block = lax.dynamic_index_in_dim(compliance_rows, index, 1, keepdims=False)
            return total + jnp.einsum(
                "tib,iab->tia", piece, block, preferred_element_type=jnp.float32
            )

        starting_total = jnp.zeros((temporal_points, number_surfaces, SURFACE_EXTENT), jnp.float32)
        operator_multiply = lax.fori_loop(0, stored_blocks, add_block, starting_total)
        proportional_reaction = (
            operator_multiply.reshape(temporal_points, segment_breadth) + applied_forces
        )
        upward_marker = (robin_sum - 2.0 * search_stiffness * proportional_reaction).reshape(
            temporal_points, number_surfaces, SURFACE_EXTENT
        )
        payload = jnp.concatenate([upward_marker, constitutive_parameters], axis=0)[None]
        neighbours = with_halo(payload, (("sub", 0),), 1)
        below_faces = neighbours[0, :, :group_size]
        above_faces = neighbours[2, :, group_size:]
        combined = jnp.concatenate([above_faces, below_faces], axis=1)
        chosen = jnp.take(combined, source, axis=1)
        opposing_surface = jnp.einsum(
            "tfy,fxy->tfx", chosen, turn_table, precision=lax.Precision.HIGHEST
        )
        motion_distribution, stress_distribution = cohesive(
            upward_marker, constitutive_parameters, opposing_surface, live_mask
        )
        present_motion = motion_distribution.reshape(temporal_points, segment_breadth)
        present_stress = stress_distribution.reshape(temporal_points, segment_breadth)
    return (present_motion.astype(jnp.bfloat16)[None], present_stress.astype(jnp.bfloat16)[None])


def solution(mesh):
    in_specs = (
        P("sub", "row", None, None, None),
        P("sub", "row", None),
        P("sub", None, "row"),
        P("sub", None, "row"),
        P("sub", None, "row"),
        P("sub", "row"),
        P("sub", "row"),
        P("sub", "row"),
        P("sub", "row", None),
    )
    out_specs = (P("sub", None, "row"), P("sub", None, "row"))
    return jax.shard_map(shards, mesh=mesh, in_specs=in_specs, out_specs=out_specs, check_vma=False)
```

profile of v0, /device:TPU:6, one launch (start us, length us, event | category | flops | bytes accessed | tf_op | source)
XLA Modules:
  0.0 213.4 jit_solution(7037482593136003585)
XLA Ops:
  1.7 9.7 %copy.62 = bf16[1,18,18,128,128]{4,3,1,2,0:T(8,128)(2,1)} copy(bf16[1,18,18,128,128]{4,3,2,1,0:T(8,128)(2,1)} %param.19) | data formatting | bytes 21233664 | tf_op args[0]
  11.5 7.7 %all-gather = bf16[1,32,4608]{2,1,0:T(8,128)(2,1)S(1)} all-gather(bf16[1,32,2304]{2,1,0:T(8,128)(2,1)S(1)} %get-tuple-element.411), channel_id=2, replica_groups=mesh['sub'=128,'row'=2] {'row'}, dimensions={2}, use_global_device_ids=true | all-gather | bytes 442368 | tf_op jit(solution)/shard_map/all_gather | solution.py:83
  19.5 38.6 %while.42 = (s32[]{:T(128)}, f32[32,18,128]{2,0,1:T(8,128)S(1)}, bf16[18,18,128,128]{3,2,0,1:T(8,128)(2,1)}, s32[18,18]{0,1:T(8,128)S(1)}, bf16[32,36,128]{2,0,1:T(8,128)(2,1)S(1)}, /*index=5*/s32[]{:T(128)}, s32[]{:T(128)}) while((s32[]{:T(128)}, f32[32,18,128]{2,0,1:T(8,128)S(1)}, bf16[18,18,128,128]{3,2,0,1:T(8,128)(2,1)}, ...), condition=%wide.region_1.0_spmd.clone, body=%wide.region_0.2_spmd.clone.sunk | while | flops 19096688 | bytes 1626539 | solution.py:95
  20.1 1.5 fusion.72
  22.3 1.5 fusion.72
  24.4 1.5 fusion.72
  26.6 1.5 fusion.72
  28.7 1.5 fusion.72
  30.9 1.5 fusion.72
  33.0 1.5 fusion.72
  35.2 1.5 fusion.72
  37.3 1.5 fusion.72
  39.5 1.5 fusion.72
  41.6 1.5 fusion.72
  43.8 1.5 fusion.72
  45.9 1.5 fusion.72
  48.1 1.5 fusion.72
  50.2 1.5 fusion.72
  52.3 1.5 fusion.72
  54.5 1.5 fusion.72
  56.6 1.5 fusion.72
  58.5 1.9 collective-permute-start.1
  60.4 9.1 %collective-permute-start = (f32[1,34,18,128]{3,1,2,0:T(8,128)S(1)}, f32[1,34,18,128]{3,1,2,0:T(8,128)S(1)}, u32[]{:S(2)}, u32[]{:S(2)}) collective-permute-start(f32[1,34,18,128]{3,1,2,0:T(8,128)S(1)} %fusion.30), channel_id=1, source_target_pairs={{2,0},{4,2},{6,4},{8,6},{10,8},{12,10},{14,12},{16,14},{18,16},{20... | collective-permute-start | bytes 940040 | tf_op jit(solution)/shard_map/ppermute | solution.py:23
  69.6 3.2 %collective-permute-done.1 = f32[1,34,18,128]{3,1,2,0:T(8,128)S(1)} collective-permute-done((f32[1,34,18,128]{3,1,2,0:T(8,128)S(1)}, f32[1,34,18,128]{3,1,2,0:T(8,128)S(1)}, u32[]{:S(2)}, u32[]{:S(2)}) %collective-permute-start.1) | collective-permute-done | bytes 313376 | tf_op jit(solution)/shard_map/ppermute | solution.py:21
  72.7 1.7 collective-permute-done
  75.1 1.7 convolution_bitcast_fusion.5
  79.6 7.3 %all_gather.10 = bf16[32,4608]{1,0:T(8,128)(2,1)S(1)} all-gather(bf16[32,2304]{1,0:T(8,128)(2,1)S(1)} %bitcast.172), channel_id=1, replica_groups=mesh['sub'=128,'row'=2] {'row'}, dimensions={1}, use_global_device_ids=true | all-gather | bytes 442368 | tf_op jit(solution)/shard_map/all_gather | solution.py:83
  86.9 38.6 %while.43 = (s32[]{:T(128)}, f32[32,18,128]{2,0,1:T(8,128)S(1)}, bf16[18,18,128,128]{3,2,0,1:T(8,128)(2,1)}, s32[18,18]{0,1:T(8,128)S(1)}, bf16[32,36,128]{2,0,1:T(8,128)(2,1)S(1)}, /*index=5*/s32[]{:T(128)}, s32[]{:T(128)}) while((s32[]{:T(128)}, f32[32,18,128]{2,0,1:T(8,128)S(1)}, bf16[18,18,128,128]{3,2,0,1:T(8,128)(2,1)}, ...), condition=%wide.region_3.6_spmd.clone, body=%wide.region_2.5_spmd.clone.sunk | while | flops 19096688 | bytes 1626539 | solution.py:95
  87.6 1.5 fusion.75
  89.7 1.5 fusion.75
  91.9 1.5 fusion.75
  94.0 1.5 fusion.75
  96.2 1.5 fusion.75
  98.3 1.5 fusion.75
  100.5 1.5 fusion.75
  102.6 1.5 fusion.75
  104.8 1.5 fusion.75
  106.9 1.5 fusion.75
  109.1 1.5 fusion.75
  111.2 1.5 fusion.75
  113.3 1.5 fusion.75
  115.5 1.5 fusion.75
  117.6 1.5 fusion.75
  119.8 1.5 fusion.75
  121.9 1.5 fusion.75
  124.1 1.5 fusion.75
  125.8 1.9 collective-permute-start.3
  127.7 7.9 %collective-permute-start.2 = (f32[1,34,18,128]{3,1,2,0:T(8,128)S(1)}, f32[1,34,18,128]{3,1,2,0:T(8,128)S(1)}, u32[]{:S(2)}, u32[]{:S(2)}) collective-permute-start(f32[1,34,18,128]{3,1,2,0:T(8,128)S(1)} %fusion.31), channel_id=1, source_target_pairs={{2,0},{4,2},{6,4},{8,6},{10,8},{12,10},{14,12},{16,14},{18,16},{20... | collective-permute-start | bytes 940040 | tf_op jit(solution)/shard_map/ppermute | solution.py:23
  135.6 3.2 %collective-permute-done.3 = f32[1,34,18,128]{3,1,2,0:T(8,128)S(1)} collective-permute-done((f32[1,34,18,128]{3,1,2,0:T(8,128)S(1)}, f32[1,34,18,128]{3,1,2,0:T(8,128)S(1)}, u32[]{:S(2)}, u32[]{:S(2)}) %collective-permute-start.3) | collective-permute-done | bytes 313376 | tf_op jit(solution)/shard_map/ppermute | solution.py:21
  138.8 1.7 collective-permute-done.2
  141.2 1.7 convolution_bitcast_fusion.4
  145.7 7.3 %all_gather.11 = bf16[32,4608]{1,0:T(8,128)(2,1)S(1)} all-gather(bf16[32,2304]{1,0:T(8,128)(2,1)S(1)} %bitcast.173), channel_id=1, replica_groups=mesh['sub'=128,'row'=2] {'row'}, dimensions={1}, use_global_device_ids=true | all-gather | bytes 442368 | tf_op jit(solution)/shard_map/all_gather | solution.py:83
  153.0 38.6 %while.44 = (s32[]{:T(128)}, f32[32,18,128]{2,0,1:T(8,128)S(1)}, bf16[18,18,128,128]{3,2,0,1:T(8,128)(2,1)}, s32[18,18]{0,1:T(8,128)S(1)}, bf16[32,36,128]{2,0,1:T(8,128)(2,1)S(1)}, /*index=5*/s32[]{:T(128)}, s32[]{:T(128)}) while((s32[]{:T(128)}, f32[32,18,128]{2,0,1:T(8,128)S(1)}, bf16[18,18,128,128]{3,2,0,1:T(8,128)(2,1)}, ...), condition=%wide.region_5.8_spmd.clone, body=%wide.region_4.7_spmd.clone.sunk | while | flops 19096688 | bytes 1626539 | solution.py:95
  153.7 1.5 fusion.78
  155.8 1.5 fusion.78
  158.0 1.5 fusion.78
  160.1 1.5 fusion.78
  162.3 1.5 fusion.78
  164.4 1.5 fusion.78
  191.8 1.9 collective-permute-start.5
  193.8 7.9 %collective-permute-start.4 = (f32[1,34,18,128]{3,1,2,0:T(8,128)S(1)}, f32[1,34,18,128]{3,1,2,0:T(8,128)S(1)}, u32[]{:S(2)}, u32[]{:S(2)}) collective-permute-start(f32[1,34,18,128]{3,1,2,0:T(8,128)S(1)} %fusion.32), channel_id=1, source_target_pairs={{2,0},{4,2},{6,4},{8,6},{10,8},{12,10},{14,12},{16,14},{18,16},{20... | collective-permute-start | bytes 940040 | tf_op jit(solution)/shard_map/ppermute | solution.py:23
  201.6 3.3 %collective-permute-done.5 = f32[1,34,18,128]{3,1,2,0:T(8,128)S(1)} collective-permute-done((f32[1,34,18,128]{3,1,2,0:T(8,128)S(1)}, f32[1,34,18,128]{3,1,2,0:T(8,128)S(1)}, u32[]{:S(2)}, u32[]{:S(2)}) %collective-permute-start.5) | collective-permute-done | bytes 313376 | tf_op jit(solution)/shard_map/ppermute | solution.py:21
  204.9 1.7 collective-permute-done.4
  207.3 1.7 convolution_bitcast_fusion.3
  (361 shorter events, 63.4 us)
Async XLA Ops:
  1.7 9.7 %copy-start.3 = (s32[1,18,18]{2,0,1:T(1,128)S(1)}, s32[1,18,18]{2,0,1:T(1,128)}, u32[]{:S(2)}) copy-start(s32[1,18,18]{2,0,1:T(1,128)} %param.20) | copy-start | bytes 3892
  1.7 56.4 %copy-start = (bf16[1,32,2304]{2,1,0:T(8,128)(2,1)S(1)}, bf16[1,32,2304]{2,1,0:T(8,128)(2,1)}, u32[]{:S(2)}) copy-start(bf16[1,32,2304]{2,1,0:T(8,128)(2,1)} %param.21) | copy-start | bytes 442372
  11.4 46.8 %copy-start.1 = (f32[1,2304]{1,0:T(1,128)S(1)}, f32[1,2304]{1,0:T(1,128)}, u32[]{:S(2)}) copy-start(f32[1,2304]{1,0:T(1,128)} %param.25) | copy-start | bytes 27652
  11.4 46.9 %copy-start.2 = (f32[1,2304]{1,0:T(1,128)S(1)}, f32[1,2304]{1,0:T(1,128)}, u32[]{:S(2)}) copy-start(f32[1,2304]{1,0:T(1,128)} %param.24) | copy-start | bytes 27652
  11.4 58.1 %copy-start.4 = (s32[1,18,128]{2,0,1:T(1,128)S(1)}, s32[1,18,128]{2,0,1:T(1,128)}, u32[]{:S(2)}) copy-start(s32[1,18,128]{2,0,1:T(1,128)} %param.27) | copy-start | bytes 27652
  11.4 58.1 %copy-start.5 = (s32[1,18]{1,0:T(1,128)S(1)}, s32[1,18]{1,0:T(1,128)}, u32[]{:S(2)}) copy-start(s32[1,18]{1,0:T(1,128)} %param.26) | copy-start | bytes 220
  58.5 14.2 %collective-permute-start.1 = (f32[1,34,18,128]{3,1,2,0:T(8,128)S(1)}, f32[1,34,18,128]{3,1,2,0:T(8,128)S(1)}, u32[]{:S(2)}, u32[]{:S(2)}) collective-permute-start(f32[1,34,18,128]{3,1,2,0:T(8,128)S(1)} %fusion.30), channel_id=1, source_target_pairs={{0,2},{2,4},{4,6},{6,8},{8,10},{10,12},{12,14},{14,16},{16,18},{18... | collective-permute-start | bytes 940040 | tf_op jit(solution)/shard_map/ppermute | solution.py:21
  60.4 14.1 %collective-permute-start = (f32[1,34,18,128]{3,1,2,0:T(8,128)S(1)}, f32[1,34,18,128]{3,1,2,0:T(8,128)S(1)}, u32[]{:S(2)}, u32[]{:S(2)}) collective-permute-start(f32[1,34,18,128]{3,1,2,0:T(8,128)S(1)} %fusion.30), channel_id=1, source_target_pairs={{2,0},{4,2},{6,4},{8,6},{10,8},{12,10},{14,12},{16,14},{18,16},{20... | collective-permute-start | bytes 940040 | tf_op jit(solution)/shard_map/ppermute | solution.py:23
  125.8 13.1 %collective-permute-start.3 = (f32[1,34,18,128]{3,1,2,0:T(8,128)S(1)}, f32[1,34,18,128]{3,1,2,0:T(8,128)S(1)}, u32[]{:S(2)}, u32[]{:S(2)}) collective-permute-start(f32[1,34,18,128]{3,1,2,0:T(8,128)S(1)} %fusion.31), channel_id=1, source_target_pairs={{0,2},{2,4},{4,6},{6,8},{8,10},{10,12},{12,14},{14,16},{16,18},{18... | collective-permute-start | bytes 940040 | tf_op jit(solution)/shard_map/ppermute | solution.py:21
  127.7 12.9 %collective-permute-start.2 = (f32[1,34,18,128]{3,1,2,0:T(8,128)S(1)}, f32[1,34,18,128]{3,1,2,0:T(8,128)S(1)}, u32[]{:S(2)}, u32[]{:S(2)}) collective-permute-start(f32[1,34,18,128]{3,1,2,0:T(8,128)S(1)} %fusion.31), channel_id=1, source_target_pairs={{2,0},{4,2},{6,4},{8,6},{10,8},{12,10},{14,12},{16,14},{18,16},{20... | collective-permute-start | bytes 940040 | tf_op jit(solution)/shard_map/ppermute | solution.py:23
  191.8 13.1 %collective-permute-start.5 = (f32[1,34,18,128]{3,1,2,0:T(8,128)S(1)}, f32[1,34,18,128]{3,1,2,0:T(8,128)S(1)}, u32[]{:S(2)}, u32[]{:S(2)}) collective-permute-start(f32[1,34,18,128]{3,1,2,0:T(8,128)S(1)} %fusion.32), channel_id=1, source_target_pairs={{0,2},{2,4},{4,6},{6,8},{8,10},{10,12},{12,14},{14,16},{16,18},{18... | collective-permute-start | bytes 940040 | tf_op jit(solution)/shard_map/ppermute | solution.py:21
  193.8 12.9 %collective-permute-start.4 = (f32[1,34,18,128]{3,1,2,0:T(8,128)S(1)}, f32[1,34,18,128]{3,1,2,0:T(8,128)S(1)}, u32[]{:S(2)}, u32[]{:S(2)}) collective-permute-start(f32[1,34,18,128]{3,1,2,0:T(8,128)S(1)} %fusion.32), channel_id=1, source_target_pairs={{2,0},{4,2},{6,4},{8,6},{10,8},{12,10},{14,12},{16,14},{18,16},{20... | collective-permute-start | bytes 940040 | tf_op jit(solution)/shard_map/ppermute | solution.py:23
where the time goes:
time: 216 us; the launch traced here: 213 us
  matrix products  87.2 us (40%)
  local copies, waits for them, and re-layouts  50.4 us (23%)
  starting transfers between devices  30.5 us (14%)
  blocking collectives  22.4 us (10%)
  waiting for transfers between devices  14.9 us (7%)
  other arithmetic  4.5 us (2%)
    dot_general x54, matrix products, add_block(): jnp.einsum('tib,iab->tia', piece, block, preferred_element_type=jnp.float32)  82 us
    gather x54, local copies, waits for them, and re-layouts, add_block(): piece = jnp.take(flexibility_tiles, column_slice, axis=1)  31 us
    ppermute x3, starting transfers between devices, with_halo(): lax.ppermute(head, axis, [((i + 1) % count, i) for i in range(ends)])  24.8 us
    all_gather x3, blocking collectives, shards(): lax.all_gather(robin_sum.astype(jnp.bfloat16), 'row', axis=1, tiled=True)  22.4 us
    unnamed x26, local copies, waits for them, and re-layouts  9.97 us
    ppermute x3, waiting for transfers between devices, with_halo(): lax.ppermute(tail, axis, [(i, (i + 1) % count) for i in range(ends)])  9.67 us
    ppermute x3, starting transfers between devices, with_halo(): lax.ppermute(tail, axis, [(i, (i + 1) % count) for i in range(ends)])  5.76 us
    ppermute x3, waiting for transfers between devices, with_halo(): lax.ppermute(head, axis, [((i + 1) % count, i) for i in range(ends)])  5.22 us
  transfers between devices with their start and end apart: 6, of which 6 were waited for; matrix products, arithmetic and copies ran while one was open for 0% of the time, Pallas kernels for 0%

commit v1 on v0

--- a/solution.py
+++ b/solution.py
@@ -1,3 +1,4 @@
+import functools
 import jax
 import jax.numpy as jnp
 from jax import lax
@@ -8,6 +9,15 @@
 search_stiffness = 1.0
 onset_jump = 0.15
 failure_jump = 1.5
+
+
+def run_trails_in(sample, axis_key):
+    return jnp.concatenate(
+        lax.all_to_all(jnp.stack([sample] * lax.axis_size(axis_key)), axis_key, 0, 0), axis=1
+    )
+
+
+groups_choose = functools.partial(run_trails_in, axis_key="row")
 
 
 def with_halo(cells, sides, width):
@@ -80,7 +90,7 @@
     present_stress = start_traction[0].astype(jnp.float32)
     for iteration in range(ITERS):
         robin_sum = present_stress + search_stiffness * present_motion
-        gathered_entries = lax.all_gather(robin_sum.astype(jnp.bfloat16), "row", axis=1, tiled=True)
+        gathered_entries = groups_choose(robin_sum.astype(jnp.bfloat16))
         flexibility_tiles = gathered_entries.reshape(temporal_points, -1, SURFACE_EXTENT)
 
         def add_block(index, total):

time: 216 us -> 224 us (1.037)
  the two profiles are of different devices: /device:TPU:6 before, /device:TPU:2 now
where the time goes in v1:
time: 224 us; the launch traced here: 221 us
  matrix products  87.2 us (39%)
  local copies, waits for them, and re-layouts  52 us (23%)
  starting transfers between devices  42.5 us (19%)
  waiting for transfers between devices  28.6 us (13%)
  other arithmetic  7.37 us (3%)
    dot_general x54, matrix products, add_block(): jnp.einsum('tib,iab->tia', piece, block, preferred_element_type=jnp.float32)  82 us
    gather x54, local copies, waits for them, and re-layouts, add_block(): piece = jnp.take(flexibility_tiles, column_slice, axis=1)  31 us
    ppermute x3, starting transfers between devices, with_halo(): lax.ppermute(head, axis, [((i + 1) % count, i) for i in range(ends)])  25.9 us
    all_to_all x3, waiting for transfers between devices, run_trails_in(): lax.all_to_all(jnp.stack([sample] * lax.axis_size(axis_key)), axis_key, 0...  13.7 us
    all_to_all x3, starting transfers between devices, run_trails_in(): lax.all_to_all(jnp.stack([sample] * lax.axis_size(axis_key)), axis_key, 0...  10.8 us
    unnamed x26, local copies, waits for them, and re-layouts  9.97 us
    ppermute x3, waiting for transfers between devices, with_halo(): lax.ppermute(tail, axis, [(i, (i + 1) % count) for i in range(ends)])  9.72 us
    ppermute x3, starting transfers between devices, with_halo(): lax.ppermute(tail, axis, [(i, (i + 1) % count) for i in range(ends)])  5.76 us
  transfers between devices with their start and end apart: 9, of which 8 were waited for; matrix products, arithmetic and copies ran while one was open for 5% of the time, Pallas kernels for 0%

profile of v1, /device:TPU:2, one launch (start us, length us, event | category | flops | bytes accessed | tf_op | source)
XLA Modules:
  0.0 221.2 jit_solution(10012757225502162354)
XLA Ops:
  2.4 3.4 %all-to-all-start = ((bf16[2,32,2304]{2,1,0:T(8,128)(2,1)}), bf16[2,32,2304]{2,1,0:T(8,128)(2,1)S(1)}, u32[]{:S(2)}, u32[]{:S(2)}) async-start(bf16[2,32,2304]{2,1,0:T(8,128)(2,1)} %pad_maximum_fusion.6), calls=%async_computation | async-start | bytes 589824 | tf_op jit(solution)/shard_map/all_to_all | solution.py:16
  6.6 9.7 %copy.58 = bf16[1,18,18,128,128]{4,3,1,2,0:T(8,128)(2,1)} copy(bf16[1,18,18,128,128]{4,3,2,1,0:T(8,128)(2,1)} %param.19) | data formatting | bytes 21233664 | tf_op args[0]
  17.1 38.6 %while.42 = (s32[]{:T(128)}, f32[32,18,128]{2,0,1:T(8,128)S(1)}, bf16[18,18,128,128]{3,2,0,1:T(8,128)(2,1)}, s32[18,18]{0,1:T(8,128)S(1)}, bf16[32,36,128]{2,0,1:T(8,128)(2,1)S(1)}, /*index=5*/s32[]{:T(128)}, s32[]{:T(128)}) while((s32[]{:T(128)}, f32[32,18,128]{2,0,1:T(8,128)S(1)}, bf16[18,18,128,128]{3,2,0,1:T(8,128)(2,1)}, ...), condition=%wide.region_1.0_spmd.clone, body=%wide.region_0.2_spmd.clone.sunk | while | flops 19096688 | bytes 1626539 | solution.py:105
  17.8 1.5 fusion.72
  19.9 1.5 fusion.72
  22.1 1.5 fusion.72
  24.2 1.5 fusion.72
  26.4 1.5 fusion.72
  28.5 1.5 fusion.72
  30.6 1.5 fusion.72
  32.8 1.5 fusion.72
  34.9 1.5 fusion.72
  37.1 1.5 fusion.72
  39.2 1.5 fusion.72
  41.4 1.5 fusion.72
  43.5 1.5 fusion.72
  45.7 1.5 fusion.72
  47.8 1.5 fusion.72
  50.0 1.5 fusion.72
  52.1 1.5 fusion.72
  54.3 1.5 fusion.72
  56.0 1.9 collective-permute-start.1
  57.9 10.2 %collective-permute-start = (f32[1,34,18,128]{3,1,2,0:T(8,128)S(1)}, f32[1,34,18,128]{3,1,2,0:T(8,128)S(1)}, u32[]{:S(2)}, u32[]{:S(2)}) collective-permute-start(f32[1,34,18,128]{3,1,2,0:T(8,128)S(1)} %fusion.30), channel_id=1, source_target_pairs={{2,0},{4,2},{6,4},{8,6},{10,8},{12,10},{14,12},{16,14},{18,16},{20... | collective-permute-start | bytes 940040 | tf_op jit(solution)/shard_map/ppermute | solution.py:33
  68.1 3.2 %collective-permute-done.1 = f32[1,34,18,128]{3,1,2,0:T(8,128)S(1)} collective-permute-done((f32[1,34,18,128]{3,1,2,0:T(8,128)S(1)}, f32[1,34,18,128]{3,1,2,0:T(8,128)S(1)}, u32[]{:S(2)}, u32[]{:S(2)}) %collective-permute-start.1) | collective-permute-done | bytes 313376 | tf_op jit(solution)/shard_map/ppermute | solution.py:31
  71.4 1.8 collective-permute-done
  73.7 1.7 convolution_bitcast_fusion.5
  79.1 3.9 %all-to-all-start.1 = ((bf16[2,32,2304]{2,1,0:T(8,128)(2,1)}), bf16[2,32,2304]{2,1,0:T(8,128)(2,1)S(1)}, u32[]{:S(2)}, u32[]{:S(2)}) async-start(bf16[2,32,2304]{2,1,0:T(8,128)(2,1)} %pad_maximum_fusion.7), calls=%async_computation.1 | async-start | bytes 589824 | tf_op jit(solution)/shard_map/all_to_all | solution.py:16
  83.0 6.9 %all-to-all-done.1 = bf16[2,32,2304]{2,1,0:T(8,128)(2,1)S(1)} async-done(((bf16[2,32,2304]{2,1,0:T(8,128)(2,1)}), bf16[2,32,2304]{2,1,0:T(8,128)(2,1)S(1)}, u32[]{:S(2)}, u32[]{:S(2)}) %all-to-all-start.1) | async-done | bytes 294944 | tf_op jit(solution)/shard_map/all_to_all | solution.py:16
  90.4 38.6 %while.43 = (s32[]{:T(128)}, f32[32,18,128]{2,0,1:T(8,128)S(1)}, bf16[18,18,128,128]{3,2,0,1:T(8,128)(2,1)}, s32[18,18]{0,1:T(8,128)S(1)}, bf16[32,36,128]{2,0,1:T(8,128)(2,1)S(1)}, /*index=5*/s32[]{:T(128)}, s32[]{:T(128)}) while((s32[]{:T(128)}, f32[32,18,128]{2,0,1:T(8,128)S(1)}, bf16[18,18,128,128]{3,2,0,1:T(8,128)(2,1)}, ...), condition=%wide.region_3.6_spmd.clone, body=%wide.region_2.5_spmd.clone.sunk | while | flops 19096688 | bytes 1626539 | solution.py:105
  91.0 1.5 fusion.75
  93.2 1.5 fusion.75
  95.3 1.5 fusion.75
  97.5 1.5 fusion.75
  99.6 1.5 fusion.75
  101.8 1.5 fusion.75
  103.9 1.5 fusion.75
  106.1 1.5 fusion.75
  108.2 1.5 fusion.75
  110.4 1.5 fusion.75
  112.5 1.5 fusion.75
  114.6 1.5 fusion.75
  116.8 1.5 fusion.75
  118.9 1.5 fusion.75
  121.1 1.5 fusion.75
  123.2 1.5 fusion.75
  125.4 1.5 fusion.75
  127.5 1.5 fusion.75
  129.2 1.9 collective-permute-start.3
  131.1 7.9 %collective-permute-start.2 = (f32[1,34,18,128]{3,1,2,0:T(8,128)S(1)}, f32[1,34,18,128]{3,1,2,0:T(8,128)S(1)}, u32[]{:S(2)}, u32[]{:S(2)}) collective-permute-start(f32[1,34,18,128]{3,1,2,0:T(8,128)S(1)} %fusion.31), channel_id=1, source_target_pairs={{2,0},{4,2},{6,4},{8,6},{10,8},{12,10},{14,12},{16,14},{18,16},{20... | collective-permute-start | bytes 940040 | tf_op jit(solution)/shard_map/ppermute | solution.py:33
  139.0 3.3 %collective-permute-done.3 = f32[1,34,18,128]{3,1,2,0:T(8,128)S(1)} collective-permute-done((f32[1,34,18,128]{3,1,2,0:T(8,128)S(1)}, f32[1,34,18,128]{3,1,2,0:T(8,128)S(1)}, u32[]{:S(2)}, u32[]{:S(2)}) %collective-permute-start.3) | collective-permute-done | bytes 313376 | tf_op jit(solution)/shard_map/ppermute | solution.py:31
  142.3 1.7 collective-permute-done.2
  144.6 1.7 convolution_bitcast_fusion.4
  150.0 3.4 %all-to-all-start.2 = ((bf16[2,32,2304]{2,1,0:T(8,128)(2,1)}), bf16[2,32,2304]{2,1,0:T(8,128)(2,1)S(1)}, u32[]{:S(2)}, u32[]{:S(2)}) async-start(bf16[2,32,2304]{2,1,0:T(8,128)(2,1)} %pad_maximum_fusion.8), calls=%async_computation.2 | async-start | bytes 589824 | tf_op jit(solution)/shard_map/all_to_all | solution.py:16
  153.4 6.8 %all-to-all-done.2 = bf16[2,32,2304]{2,1,0:T(8,128)(2,1)S(1)} async-done(((bf16[2,32,2304]{2,1,0:T(8,128)(2,1)}), bf16[2,32,2304]{2,1,0:T(8,128)(2,1)S(1)}, u32[]{:S(2)}, u32[]{:S(2)}) %all-to-all-start.2) | async-done | bytes 294944 | tf_op jit(solution)/shard_map/all_to_all | solution.py:16
  160.8 38.6 %while.44 = (s32[]{:T(128)}, f32[32,18,128]{2,0,1:T(8,128)S(1)}, bf16[18,18,128,128]{3,2,0,1:T(8,128)(2,1)}, s32[18,18]{0,1:T(8,128)S(1)}, bf16[32,36,128]{2,0,1:T(8,128)(2,1)S(1)}, /*index=5*/s32[]{:T(128)}, s32[]{:T(128)}) while((s32[]{:T(128)}, f32[32,18,128]{2,0,1:T(8,128)S(1)}, bf16[18,18,128,128]{3,2,0,1:T(8,128)(2,1)}, ...), condition=%wide.region_5.8_spmd.clone, body=%wide.region_4.7_spmd.clone.sunk | while | flops 19096688 | bytes 1626539 | solution.py:105
  161.5 1.5 fusion.78
  163.6 1.5 fusion.78
  165.8 1.5 fusion.78
  182.9 1.5 fusion.78
  199.6 1.9 collective-permute-start.5
  201.6 7.9 %collective-permute-start.4 = (f32[1,34,18,128]{3,1,2,0:T(8,128)S(1)}, f32[1,34,18,128]{3,1,2,0:T(8,128)S(1)}, u32[]{:S(2)}, u32[]{:S(2)}) collective-permute-start(f32[1,34,18,128]{3,1,2,0:T(8,128)S(1)} %fusion.32), channel_id=1, source_target_pairs={{2,0},{4,2},{6,4},{8,6},{10,8},{12,10},{14,12},{16,14},{18,16},{20... | collective-permute-start | bytes 940040 | tf_op jit(solution)/shard_map/ppermute | solution.py:33
  209.4 3.3 %collective-permute-done.5 = f32[1,34,18,128]{3,1,2,0:T(8,128)S(1)} collective-permute-done((f32[1,34,18,128]{3,1,2,0:T(8,128)S(1)}, f32[1,34,18,128]{3,1,2,0:T(8,128)S(1)}, u32[]{:S(2)}, u32[]{:S(2)}) %collective-permute-start.5) | collective-permute-done | bytes 313376 | tf_op jit(solution)/shard_map/ppermute | solution.py:31
  212.7 1.7 collective-permute-done.4
  215.1 1.7 convolution_bitcast_fusion.3
  (374 shorter events, 70.9 us)
Async XLA Ops:
  2.4 14.2 %all-to-all-start = ((bf16[2,32,2304]{2,1,0:T(8,128)(2,1)}), bf16[2,32,2304]{2,1,0:T(8,128)(2,1)S(1)}, u32[]{:S(2)}, u32[]{:S(2)}) async-start(bf16[2,32,2304]{2,1,0:T(8,128)(2,1)} %pad_maximum_fusion.6), calls=%async_computation | async-start | bytes 589824 | tf_op jit(solution)/shard_map/all_to_all | solution.py:16
  6.6 9.8 %copy-start.3 = (s32[1,18,18]{2,0,1:T(1,128)S(1)}, s32[1,18,18]{2,0,1:T(1,128)}, u32[]{:S(2)}) copy-start(s32[1,18,18]{2,0,1:T(1,128)} %param.20) | copy-start | bytes 3892
  6.6 9.8 %copy-start = (bf16[1,32,2304]{2,1,0:T(8,128)(2,1)S(1)}, bf16[1,32,2304]{2,1,0:T(8,128)(2,1)}, u32[]{:S(2)}) copy-start(bf16[1,32,2304]{2,1,0:T(8,128)(2,1)} %param.21) | copy-start | bytes 442372
  6.6 9.9 %copy-start.4 = (s32[1,18,128]{2,0,1:T(1,128)S(1)}, s32[1,18,128]{2,0,1:T(1,128)}, u32[]{:S(2)}) copy-start(s32[1,18,128]{2,0,1:T(1,128)} %param.27) | copy-start | bytes 27652
  6.6 9.9 %copy-start.1 = (f32[1,2304]{1,0:T(1,128)S(1)}, f32[1,2304]{1,0:T(1,128)}, u32[]{:S(2)}) copy-start(f32[1,2304]{1,0:T(1,128)} %param.25) | copy-start | bytes 27652
  6.6 9.9 %copy-start.2 = (f32[1,2304]{1,0:T(1,128)S(1)}, f32[1,2304]{1,0:T(1,128)}, u32[]{:S(2)}) copy-start(f32[1,2304]{1,0:T(1,128)} %param.24) | copy-start | bytes 27652
  16.3 41.6 %copy-start.5 = (s32[1,18]{1,0:T(1,128)S(1)}, s32[1,18]{1,0:T(1,128)}, u32[]{:S(2)}) copy-start(s32[1,18]{1,0:T(1,128)} %param.26) | copy-start | bytes 220
  56.0 15.4 %collective-permute-start.1 = (f32[1,34,18,128]{3,1,2,0:T(8,128)S(1)}, f32[1,34,18,128]{3,1,2,0:T(8,128)S(1)}, u32[]{:S(2)}, u32[]{:S(2)}) collective-permute-start(f32[1,34,18,128]{3,1,2,0:T(8,128)S(1)} %fusion.30), channel_id=1, source_target_pairs={{0,2},{2,4},{4,6},{6,8},{8,10},{10,12},{12,14},{14,16},{16,18},{18... | collective-permute-start | bytes 940040 | tf_op jit(solution)/shard_map/ppermute | solution.py:31
  57.9 15.2 %collective-permute-start = (f32[1,34,18,128]{3,1,2,0:T(8,128)S(1)}, f32[1,34,18,128]{3,1,2,0:T(8,128)S(1)}, u32[]{:S(2)}, u32[]{:S(2)}) collective-permute-start(f32[1,34,18,128]{3,1,2,0:T(8,128)S(1)} %fusion.30), channel_id=1, source_target_pairs={{2,0},{4,2},{6,4},{8,6},{10,8},{12,10},{14,12},{16,14},{18,16},{20... | collective-permute-start | bytes 940040 | tf_op jit(solution)/shard_map/ppermute | solution.py:33
  79.1 10.8 %all-to-all-start.1 = ((bf16[2,32,2304]{2,1,0:T(8,128)(2,1)}), bf16[2,32,2304]{2,1,0:T(8,128)(2,1)S(1)}, u32[]{:S(2)}, u32[]{:S(2)}) async-start(bf16[2,32,2304]{2,1,0:T(8,128)(2,1)} %pad_maximum_fusion.7), calls=%async_computation.1 | async-start | bytes 589824 | tf_op jit(solution)/shard_map/all_to_all | solution.py:16
  129.2 13.1 %collective-permute-start.3 = (f32[1,34,18,128]{3,1,2,0:T(8,128)S(1)}, f32[1,34,18,128]{3,1,2,0:T(8,128)S(1)}, u32[]{:S(2)}, u32[]{:S(2)}) collective-permute-start(f32[1,34,18,128]{3,1,2,0:T(8,128)S(1)} %fusion.31), channel_id=1, source_target_pairs={{0,2},{2,4},{4,6},{6,8},{8,10},{10,12},{12,14},{14,16},{16,18},{18... | collective-permute-start | bytes 940040 | tf_op jit(solution)/shard_map/ppermute | solution.py:31
  131.1 12.9 %collective-permute-start.2 = (f32[1,34,18,128]{3,1,2,0:T(8,128)S(1)}, f32[1,34,18,128]{3,1,2,0:T(8,128)S(1)}, u32[]{:S(2)}, u32[]{:S(2)}) collective-permute-start(f32[1,34,18,128]{3,1,2,0:T(8,128)S(1)} %fusion.31), channel_id=1, source_target_pairs={{2,0},{4,2},{6,4},{8,6},{10,8},{12,10},{14,12},{16,14},{18,16},{20... | collective-permute-start | bytes 940040 | tf_op jit(solution)/shard_map/ppermute | solution.py:33
  150.0 10.3 %all-to-all-start.2 = ((bf16[2,32,2304]{2,1,0:T(8,128)(2,1)}), bf16[2,32,2304]{2,1,0:T(8,128)(2,1)S(1)}, u32[]{:S(2)}, u32[]{:S(2)}) async-start(bf16[2,32,2304]{2,1,0:T(8,128)(2,1)} %pad_maximum_fusion.8), calls=%async_computation.2 | async-start | bytes 589824 | tf_op jit(solution)/shard_map/all_to_all | solution.py:16
  199.6 13.1 %collective-permute-start.5 = (f32[1,34,18,128]{3,1,2,0:T(8,128)S(1)}, f32[1,34,18,128]{3,1,2,0:T(8,128)S(1)}, u32[]{:S(2)}, u32[]{:S(2)}) collective-permute-start(f32[1,34,18,128]{3,1,2,0:T(8,128)S(1)} %fusion.32), channel_id=1, source_target_pairs={{0,2},{2,4},{4,6},{6,8},{8,10},{10,12},{12,14},{14,16},{16,18},{18... | collective-permute-start | bytes 940040 | tf_op jit(solution)/shard_map/ppermute | solution.py:31
  201.6 12.9 %collective-permute-start.4 = (f32[1,34,18,128]{3,1,2,0:T(8,128)S(1)}, f32[1,34,18,128]{3,1,2,0:T(8,128)S(1)}, u32[]{:S(2)}, u32[]{:S(2)}) collective-permute-start(f32[1,34,18,128]{3,1,2,0:T(8,128)S(1)} %fusion.32), channel_id=1, source_target_pairs={{2,0},{4,2},{6,4},{8,6},{10,8},{12,10},{14,12},{16,14},{18,16},{20... | collective-permute-start | bytes 940040 | tf_op jit(solution)/shard_map/ppermute | solution.py:33
